TPU v7x, 128 devices: a whole 4x4x4 slice. The times are simulated.
128 devices in a mesh: ctx: 16 (over y_hi, x, core), tp: 8 (over y_lo, z).
Axes of the slice: x: 4, y: 4 (y_hi: 2, y_lo: 2; y = y_hi * 2 + y_lo), z: 4, core: 2. Of those that a mesh axis runs over, the one named last changes fastest.
Arguments:
- tokens: bfloat16 [2048, 4096], P('ctx', 'tp'), may hold values from -6 to 6
- in_weight: bfloat16 [4096, 3, 4096], P(None, None, 'tp'), may hold values from -0.09375 to 0.09375
- conv_weight: float32 [7, 3, 4096], P(None, None, 'tp'), may hold values from -2 to 2
- filters: bfloat16 [2048, 4096], P(None, 'tp'), may hold values from -1 to 1
- skip_gain: float32 [4096], P('tp'), may hold values from -4 to 4
Outputs:
- mixed_out: bfloat16 [2048, 4096], P('ctx', 'tp')
All inputs are finite; a program needn't handle non-finite values.
Results may differ from a plain program's by a relative error of at most 0.0095.
Values may be sent and summed in bfloat16 or wider, within the bound.
A program may use at most 128 MiB of HBM per device.

v0:
```python
import math
import jax
import jax.numpy as jnp
from jax import lax
from jax.sharding import PartitionSpec as P

TAPS = 7


def passed_along(value, axis, steps):
    count = lax.axis_size(axis)
    leading, last = (max(0, -steps), min(count, count - steps))
    return lax.ppermute(value, axis, [(source, source + steps) for source in range(leading, last)])


def exact_dot(left, right):
    return jnp.dot(left, right, precision=lax.Precision.HIGHEST, preferred_element_type=jnp.float32)


def split_table(table):
    high = table.astype(jnp.bfloat16)
    low = (table - high.astype(jnp.float32)).astype(jnp.bfloat16)
    return (high, low)


def local(tokens, in_weight, conv_weight, filters, skip_gain):
    block_rows = tokens.shape[0]
    channels = in_weight.shape[2]
    flat_weight = in_weight.reshape(in_weight.shape[0], 3 * channels)
    gathered = lax.all_gather(tokens, "tp", axis=1, tiled=True)
    summed = jnp.dot(gathered, flat_weight, preferred_element_type=jnp.float32)
    projected = summed.astype(jnp.bfloat16).reshape(block_rows, 3, channels)
    earlier = passed_along(projected[block_rows - (TAPS - 1) :], "ctx", 1)
    extended = jnp.concatenate([earlier, projected], 0).astype(jnp.float32)
    branches = conv_weight[0] * extended[0:block_rows]
    for tap_index in range(1, TAPS):
        branches = branches + conv_weight[tap_index] * extended[tap_index : tap_index + block_rows]
    gate_branch = branches[:, 0]
    product = (branches[:, 1] * branches[:, 2]).astype(jnp.bfloat16)
    product_wide = product.astype(jnp.float32)
    sub_rows = block_rows // 2
    dft_length = 2 * sub_rows
    frequency = jnp.arange(sub_rows, dtype=jnp.int32)
    position = jnp.arange(sub_rows, dtype=jnp.int32)
    step_angle = 2.0 * math.pi / dft_length
    angles = (frequency[:, None] * position[None, :] % dft_length).astype(jnp.float32) * step_angle
    cos_high, cos_low = split_table(jnp.cos(angles))
    sin_high, sin_low = split_table(-jnp.sin(angles))
    alternate = jnp.where(frequency % 2 == 0, 1.0, -1.0).astype(jnp.float32)[:, None]
    nyquist_sign = jnp.where(position % 2 == 0, 1.0, -1.0).astype(jnp.bfloat16)
    nyquist_alternate = 1.0
    back_angles = ((position[:, None] + sub_rows) * frequency[None, :] % dft_length).astype(
        jnp.float32
    ) * step_angle
    back_weights = jnp.where(frequency == 0, 1.0, 2.0).astype(jnp.float32)[None, :]
    cos_back = jnp.cos(back_angles) * back_weights
    sin_back = jnp.sin(back_angles) * back_weights
    nyquist_back = jnp.where((position + sub_rows) % 2 == 0, 1.0, -1.0).astype(jnp.float32)

    def spectrum(data):
        real_part = jnp.einsum(
            "ks,hsc->hkc", cos_high, data, preferred_element_type=jnp.float32
        ) + jnp.einsum("ks,hsc->hkc", cos_low, data, preferred_element_type=jnp.float32)
        imag_part = jnp.einsum(
            "ks,hsc->hkc", sin_high, data, preferred_element_type=jnp.float32
        ) + jnp.einsum("ks,hsc->hkc", sin_low, data, preferred_element_type=jnp.float32)
        nyquist = jnp.einsum("s,hsc->hc", nyquist_sign, data, preferred_element_type=jnp.float32)
        return (real_part, imag_part, nyquist)

    blocks = filters.shape[0] // sub_rows
    filter_real, filter_imag, filter_nyquist = spectrum(filters.reshape(blocks, sub_rows, channels))
    padded_real = jnp.concatenate([jnp.zeros((1, sub_rows, channels), jnp.float32), filter_real], 0)
    padded_imag = jnp.concatenate([jnp.zeros((1, sub_rows, channels), jnp.float32), filter_imag], 0)
    padded_nyquist = jnp.concatenate([jnp.zeros((1, channels), jnp.float32), filter_nyquist], 0)
    own_index = lax.axis_index("ctx")

    def gain_at(distance):
        causal = (distance >= 0).astype(jnp.float32)
        lag_index = jnp.clip(distance, 0, blocks - 1)
        gain_real = lax.dynamic_index_in_dim(
            padded_real, lag_index, 0, keepdims=False
        ) + alternate * lax.dynamic_index_in_dim(padded_real, lag_index + 1, 0, keepdims=False)
        gain_imag = lax.dynamic_index_in_dim(
            padded_imag, lag_index, 0, keepdims=False
        ) + alternate * lax.dynamic_index_in_dim(padded_imag, lag_index + 1, 0, keepdims=False)
        gain_nyquist = lax.dynamic_index_in_dim(
            padded_nyquist, lag_index, 0, keepdims=False
        ) + nyquist_alternate * lax.dynamic_index_in_dim(
            padded_nyquist, lag_index + 1, 0, keepdims=False
        )
        return (causal * gain_real, causal * gain_imag, causal * gain_nyquist)

    def add_term(running, source_real, source_imag, source_nyquist, source_block):
        next_real, next_imag, next_nyquist = ([], [], [])
        for target in range(2):
            total_real = running[0][target]
            total_imag = running[1][target]
            total_nyquist = running[2][target]
            for half in range(2):
                gain_real, gain_imag, gain_nyquist = gain_at(
                    2 * (own_index - source_block) + target - half
                )
                total_real = (
                    total_real + gain_real * source_real[half] - gain_imag * source_imag[half]
                )
                total_imag = (
                    total_imag + gain_real * source_imag[half] + gain_imag * source_real[half]
                )
                total_nyquist = total_nyquist + gain_nyquist * source_nyquist[half]
            next_real.append(total_real)
            next_imag.append(total_imag)
            next_nyquist.append(total_nyquist)
        return (jnp.stack(next_real), jnp.stack(next_imag), jnp.stack(next_nyquist))

    initial = (
        jnp.zeros((2, sub_rows, channels), jnp.float32),
        jnp.zeros((2, sub_rows, channels), jnp.float32),
        jnp.zeros((2, channels), jnp.float32),
    )
    shard_part = lax.all_gather(product[None], "ctx", axis=0, tiled=True)

    def visit_member(member, state):
        block_data = lax.dynamic_index_in_dim(shard_part, member, 0, keepdims=False).reshape(
            2, sub_rows, channels
        )
        source_real, source_imag, source_nyquist = spectrum(block_data)
        return add_term(state, source_real, source_imag, source_nyquist, member)

    totals = lax.fori_loop(0, shard_part.shape[0], visit_member, initial)
    halves = []
    for target in range(2):
        halves.append(
            exact_dot(cos_back, totals[0][target])
            - exact_dot(sin_back, totals[1][target])
            + nyquist_back[:, None] * totals[2][target][None, :]
        )
    convolved = jnp.concatenate(halves, 0) / dft_length
    return (gate_branch * (convolved + skip_gain * product_wide)).astype(jnp.bfloat16)


def solution(mesh):
    placed = (P("ctx", "tp"), P(None, None, "tp"), P(None, None, "tp"), P(None, "tp"), P("tp"))
    return jax.shard_map(
        local, mesh=mesh, in_specs=placed, out_specs=P("ctx", "tp"), check_vma=False
    )
```

profile of v0, /device:TPU:1, one launch (start us, length us, event | category | flops | bytes accessed | tf_op | source)
XLA Modules:
  0.0 261.4 jit_solution(9611068512065455228)
XLA Ops:
  7.3 17.0 %copy.8 = bf16[4096,3,512]{0,2,1:T(8,128)(2,1)} copy(bf16[4096,3,512]{2,0,1:T(8,128)(2,1)} %param.8) | data formatting | bytes 25165824 | tf_op args[1]
  24.3 22.3 %all-gather.4.cloned.1.call-done = bf16[128,4096]{1,0:T(8,128)(2,1)} async-done(((bf16[128,512]{1,0:T(8,128)(2,1)}), bf16[128,4096]{1,0:T(8,128)(2,1)}) %all-gather.4.cloned.1.call-update) | async-done | bytes 1048592 | tf_op jit(solution)/shard_map/all_gather | solution.py:30
  46.7 9.2 %convolution_convert_fusion = bf16[128,1536]{1,0:T(8,128)(2,1)S(1)} fusion(bf16[128,4096]{1,0:T(8,128)(2,1)} %all-gather.4.cloned.1.call-done, bf16[4096,1536]{0,1:T(8,128)(2,1)} %bitcast.142), kind=kOutput, calls=%fused_computation.99 | convolution fusion | flops 1610809344 | bytes 14024704 | tf_op jit(solution)/shard_map/dot_general | solution.py:31
  55.9 8.4 %collective-permute-start = (bf16[6,3,512]{2,0,1:T(8,128)(2,1)S(1)}, bf16[6,3,512]{2,0,1:T(8,128)(2,1)S(1)}, u32[]{:S(2)}, u32[]{:S(2)}) collective-permute-start(bf16[6,3,512]{2,0,1:T(8,128)(2,1)S(1)} %bitcast.148), channel_id=1, source_target_pairs={{0,8},{8,16},{16,24},{24,32},{32,40},{40,48},{48,56},{56,64},{64,7... | collective-permute-start | bytes 55304 | tf_op jit(solution)/shard_map/ppermute | solution.py:13
  69.6 2.6 concatenate.16
  73.8 2.6 %concatenate.17 = f32[33,64,512]{2,1,0:T(8,128)} pad(f32[32,64,512]{2,1,0:T(8,128)S(1)} %add_bitcast_fusion, f32[]{:T(128)} %constant.212.clone.1), padding=1_0x0_0x0_0 | pad | bytes 8519684 | tf_op jit(solution)/shard_map/concatenate | solution.py:73
  77.7 39.6 %all-gather.6.cloned.1.call-done = bf16[2048,1,512]{2,0,1:T(8,128)(2,1)} async-done(((bf16[128,1,512]{2,0,1:T(8,128)(2,1)}), bf16[2048,1,512]{2,0,1:T(8,128)(2,1)}) %all-gather.6.cloned.1.call-update) | async-done | bytes 2097168 | tf_op jit(solution)/shard_map/all_gather | solution.py:120
  118.1 130.9 %while.24 = (s32[]{:T(128)}, f32[2,64,512]{2,1,0:T(8,128)S(1)}, f32[2,64,512]{2,1,0:T(8,128)}, f32[2,512]{1,0:T(2,128)S(1)}, s32[]{:T(128)}, /*index=5*/f32[33,6...) while((s32[]{:T(128)}, f32[2,64,512]{2,1,0:T(8,128)S(1)}, ...), condition=%wide.region_1.2_spmd.clone.clone, body=%wide.region_0.1_spmd.clone.clone.sunk | while | flops 36070464 | bytes 9090577 | solution.py:129
  120.2 1.6 multiply_add_fusion.5
  121.8 1.2 multiply_subtract_fusion.3
  123.0 1.4 multiply_add_fusion.6
  128.4 1.6 multiply_add_fusion.5
  129.9 1.2 multiply_subtract_fusion.3
  131.2 1.4 multiply_add_fusion.6
  133.4 1.0 add_add_fusion.2
  136.6 1.6 multiply_add_fusion.5
  138.1 1.2 multiply_subtract_fusion.3
  139.4 1.4 multiply_add_fusion.6
  141.6 1.0 add_add_fusion.2
  144.7 1.6 multiply_add_fusion.5
  146.3 1.2 multiply_subtract_fusion.3
  147.6 1.4 multiply_add_fusion.6
  149.8 1.0 add_add_fusion.2
  152.9 1.6 multiply_add_fusion.5
  154.5 1.2 multiply_subtract_fusion.3
  155.7 1.4 multiply_add_fusion.6
  161.1 1.6 multiply_add_fusion.5
  162.7 1.2 multiply_subtract_fusion.3
  163.9 1.4 multiply_add_fusion.6
  169.3 1.6 multiply_add_fusion.5
  170.9 1.2 multiply_subtract_fusion.3
  172.1 1.4 multiply_add_fusion.6
  177.5 1.6 multiply_add_fusion.5
  179.1 1.2 multiply_subtract_fusion.3
  180.3 1.4 multiply_add_fusion.6
  182.5 1.0 add_add_fusion.2
  185.7 1.6 multiply_add_fusion.5
  187.2 1.2 multiply_subtract_fusion.3
  188.5 1.4 multiply_add_fusion.6
  190.7 1.0 add_add_fusion.2
  193.9 1.6 multiply_add_fusion.5
  195.4 1.2 multiply_subtract_fusion.3
  196.7 1.4 multiply_add_fusion.6
  202.0 1.6 multiply_add_fusion.5
  203.6 1.2 multiply_subtract_fusion.3
  204.9 1.4 multiply_add_fusion.6
  210.2 1.6 multiply_add_fusion.5
  211.8 1.2 multiply_subtract_fusion.3
  213.0 1.4 multiply_add_fusion.6
  218.4 1.6 multiply_add_fusion.5
  220.0 1.2 multiply_subtract_fusion.3
  221.2 1.4 multiply_add_fusion.6
  226.6 1.6 multiply_add_fusion.5
  228.2 1.2 multiply_subtract_fusion.3
  229.4 1.4 multiply_add_fusion.6
  234.8 1.6 multiply_add_fusion.5
  236.4 1.2 multiply_subtract_fusion.3
  237.6 1.4 multiply_add_fusion.6
  243.0 1.6 multiply_add_fusion.5
  244.5 1.2 multiply_subtract_fusion.3
  245.8 1.4 multiply_add_fusion.6
  249.9 1.3 fusion.77
  251.3 1.4 fusion.78
  252.6 1.9 fusion.87
  (208 shorter events, 68.4 us)
Async XLA Ops:
  6.5 61.1 %copy-start = (bf16[2048,512]{1,0:T(8,128)(2,1)S(1)}, bf16[2048,512]{1,0:T(8,128)(2,1)}, u32[]{:S(2)}) copy-start(bf16[2048,512]{1,0:T(8,128)(2,1)} %param.10) | copy-start | bytes 6291460
  6.5 40.1 %all-gather.4.cloned.1.call-start = ((), (), s32[]{:S(2)}) async-start(), calls=%async_computation | async-start | bytes 1179648 | tf_op jit(solution)/shard_map/all_gather | solution.py:30
  7.3 17.0 %copy-start.2 = (f32[7,3,512]{2,0,1:T(8,128)S(1)}, f32[7,3,512]{2,0,1:T(8,128)}, u32[]{:S(2)}) copy-start(f32[7,3,512]{2,0,1:T(8,128)} %param.9) | copy-start | bytes 129028
  7.3 110.1 %all-gather.6.cloned.1.call-start = ((), (), s32[]{:S(2)}) async-start(), calls=%async_computation.1 | async-start | bytes 2228224 | tf_op jit(solution)/shard_map/all_gather | solution.py:120
  55.9 9.4 %collective-permute-start = (bf16[6,3,512]{2,0,1:T(8,128)(2,1)S(1)}, bf16[6,3,512]{2,0,1:T(8,128)(2,1)S(1)}, u32[]{:S(2)}, u32[]{:S(2)}) collective-permute-start(bf16[6,3,512]{2,0,1:T(8,128)(2,1)S(1)} %bitcast.148), channel_id=1, source_target_pairs={{0,8},{8,16},{16,24},{24,32},{32,40},{40,48},{48,56},{56,64},{64,7... | collective-permute-start | bytes 55304 | tf_op jit(solution)/shard_map/ppermute | solution.py:13
  66.0 0.9 copy-start.1
Sparse Core Ops, SparseCore 0:
  9.0 37.5 all-gather.3
  67.7 49.5 all-gather.5
where the time goes:
time: 264 us; the launch traced here: 261 us
  other arithmetic  97.9 us (37%)
  waiting for transfers between devices  63.2 us (24%)
  local copies, waits for them, and re-layouts  39.7 us (15%)
  matrix products  36.7 us (14%)
  between operations  13.6 us (5%)
  starting transfers between devices  8.48 us (3%)
    add x32, other arithmetic, add_term(): total_imag + gain_real * source_imag[half] + gain_imag * source_real[half]  46.9 us
    all_gather x1, waiting for transfers between devices, local(): shard_part = lax.all_gather(product[None], 'ctx', axis=0, tiled=True)  39.6 us
    all_gather x1, waiting for transfers between devices, local(): gathered = lax.all_gather(tokens, 'tp', axis=1, tiled=True)  22.3 us
    sub x16, other arithmetic, add_term(): total_real + gain_real * source_real[half] - gain_imag * source_imag[half]  19.5 us
    unnamed x11, local copies, waits for them, and re-layouts  17.9 us
    add x16, other arithmetic, add_term(): total_nyquist = total_nyquist + gain_nyquist * source_nyquist[half]  15.4 us
    dynamic_slice x16, local copies, waits for them, and re-layouts, visit_member(): lax.dynamic_index_in_dim(shard_part, member, 0, keepdims=False)  14.7 us
    another operation x32, other arithmetic, add_term(): return (jnp.stack(next_real), jnp.stack(next_imag), jnp.stack(next_nyquist))  12 us
  transfers between devices with their start and end apart: 3, of which 3 were waited for; matrix products, arithmetic and copies ran while one was open for 11% of the time, Pallas kernels for 0%

commit v1 on v0

--- a/solution.py
+++ b/solution.py
@@ -27,7 +27,9 @@
     block_rows = tokens.shape[0]
     channels = in_weight.shape[2]
     flat_weight = in_weight.reshape(in_weight.shape[0], 3 * channels)
-    gathered = lax.all_gather(tokens, "tp", axis=1, tiled=True)
+    gathered = jnp.concatenate(
+        lax.all_to_all(jnp.stack([tokens] * lax.axis_size("tp")), "tp", 0, 0), axis=1
+    )
     summed = jnp.dot(gathered, flat_weight, preferred_element_type=jnp.float32)
     projected = summed.astype(jnp.bfloat16).reshape(block_rows, 3, channels)
     earlier = passed_along(projected[block_rows - (TAPS - 1) :], "ctx", 1)

time: 264 us -> 249 us (0.943)
  waiting for transfers between devices: 63.2 us -> 41.4 us
  local copies, waits for them, and re-layouts: 39.7 us -> 43.8 us
    all_gather x1 -> x0, waiting for transfers between devices: 22.3 us -> none  [local(): gathered = lax.all_gather(tokens, 'tp', axis=1, tiled=True)]
    all_to_all x0 -> x1, starting transfers between devices: none -> 6.88 us  [local(): lax.all_to_all(jnp.stack([tokens] * lax.axis_size('tp')), 'tp', 0, 0)]
    ppermute x1, starting transfers between devices: 8.43 us -> 4.13 us  [passed_along(): lax.ppermute(value, axis, [(source, source + steps) for source in range(l...]
    unnamed x11 -> x14, local copies, waits for them, and re-layouts: 17.9 us -> 19.8 us
  transfers between devices with their start and end apart: 3 -> 3, of which waited for: 3 -> 1; matrix products, arithmetic and copies ran while one was open for 11% -> 12% of each run, Pallas kernels for 0% -> 0%
where the time goes in v1:
time: 249 us; the launch traced here: 246 us
  other arithmetic  98 us (39%)
  local copies, waits for them, and re-layouts  43.8 us (18%)
  waiting for transfers between devices  41.4 us (17%)
  matrix products  36.3 us (15%)
  between operations  13.6 us (5%)
  starting transfers between devices  11.1 us (4%)
    add x32, other arithmetic, add_term(): total_imag + gain_real * source_imag[half] + gain_imag * source_real[half]  46.9 us
    all_gather x1, waiting for transfers between devices, local(): shard_part = lax.all_gather(product[None], 'ctx', axis=0, tiled=True)  41.4 us
    unnamed x14, local copies, waits for them, and re-layouts  19.8 us
    sub x16, other arithmetic, add_term(): total_real + gain_real * source_real[half] - gain_imag * source_imag[half]  19.5 us
    add x16, other arithmetic, add_term(): total_nyquist = total_nyquist + gain_nyquist * source_nyquist[half]  15.4 us
    dynamic_slice x16, local copies, waits for them, and re-layouts, visit_member(): lax.dynamic_index_in_dim(shard_part, member, 0, keepdims=False)  14.7 us
    another operation x32, other arithmetic, add_term(): return (jnp.stack(next_real), jnp.stack(next_imag), jnp.stack(next_nyquist))  12.1 us
    dot_general x1, matrix products, local(): summed = jnp.dot(gathered, flat_weight, preferred_element_type=jnp.float32)  8.88 us
  transfers between devices with their start and end apart: 3, of which 1 were waited for; matrix products, arithmetic and copies ran while one was open for 12% of the time, Pallas kernels for 0%

profile of v1, /device:TPU:1, one launch (start us, length us, event | category | flops | bytes accessed | tf_op | source)
XLA Modules:
  0.0 245.9 jit_solution(12972545775239337957)
XLA Ops:
  6.5 1.2 copy.8
  7.7 1.2 stack.71
  8.9 6.9 %all-to-all-start = ((bf16[8,128,512]{1,2,0:T(8,128)(2,1)}), bf16[8,128,512]{1,2,0:T(8,128)(2,1)S(1)}, u32[]{:S(2)}, u32[]{:S(2)}) async-start(bf16[8,128,512]{1,2,0:T(8,128)(2,1)} %stack.71), calls=%async_computation | async-start | bytes 2097152 | tf_op jit(solution)/shard_map/all_to_all | solution.py:31
  15.8 17.0 %copy.9 = bf16[4096,3,512]{0,2,1:T(8,128)(2,1)} copy(bf16[4096,3,512]{2,0,1:T(8,128)(2,1)} %param.8) | data formatting | bytes 25165824 | tf_op args[1]
  32.8 8.9 %convolution_convert_fusion = bf16[128,1536]{1,0:T(8,128)(2,1)S(1)} fusion(bf16[128,4096]{0,1:T(8,128)(2,1)S(1)} %bitcast.146, bf16[4096,1536]{0,1:T(8,128)(2,1)} %bitcast.145), kind=kOutput, calls=%fused_computation.99 | convolution fusion | flops 1610809344 | bytes 14024704 | tf_op jit(solution)/shard_map/dot_general | solution.py:33
  42.5 4.1 %collective-permute-start = (bf16[6,3,512]{2,0,1:T(8,128)(2,1)S(1)}, bf16[6,3,512]{2,0,1:T(8,128)(2,1)S(1)}, u32[]{:S(2)}, u32[]{:S(2)}) collective-permute-start(bf16[6,3,512]{2,0,1:T(8,128)(2,1)S(1)} %bitcast.152), channel_id=1, source_target_pairs={{0,8},{8,16},{16,24},{24,32},{32,40},{40,48},{48,56},{56,64},{64,7... | collective-permute-start | bytes 55304 | tf_op jit(solution)/shard_map/ppermute | solution.py:13
  46.7 1.2 copy.11
  52.5 2.6 %concatenate.16 = f32[33,64,512]{2,1,0:T(8,128)} pad(f32[32,64,512]{2,1,0:T(8,128)S(1)} %add_bitcast_fusion.1, f32[]{:T(128)} %constant.212.clone.1), padding=1_0x0_0x0_0 | pad | bytes 8519684 | tf_op jit(solution)/shard_map/concatenate | solution.py:74
  56.7 2.6 %concatenate.17 = f32[33,64,512]{2,1,0:T(8,128)} pad(f32[32,64,512]{2,1,0:T(8,128)S(1)} %add_bitcast_fusion, f32[]{:T(128)} %constant.212.clone.1), padding=1_0x0_0x0_0 | pad | bytes 8519684 | tf_op jit(solution)/shard_map/concatenate | solution.py:75
  60.5 41.4 %all-gather.3.cloned.1.call-done = bf16[2048,1,512]{2,0,1:T(8,128)(2,1)} async-done(((bf16[128,1,512]{2,0,1:T(8,128)(2,1)}), bf16[2048,1,512]{2,0,1:T(8,128)(2,1)}) %all-gather.3.cloned.1.call-update) | async-done | bytes 2097168 | tf_op jit(solution)/shard_map/all_gather | solution.py:122
  102.7 130.9 %while.24 = (s32[]{:T(128)}, f32[2,64,512]{2,1,0:T(8,128)S(1)}, f32[2,64,512]{2,1,0:T(8,128)}, f32[2,512]{1,0:T(2,128)S(1)}, s32[]{:T(128)}, /*index=5*/f32[33,6...) while((s32[]{:T(128)}, f32[2,64,512]{2,1,0:T(8,128)S(1)}, ...), condition=%wide.region_1.2_spmd.clone.clone, body=%wide.region_0.1_spmd.clone.clone.sunk | while | flops 36070464 | bytes 9090577 | solution.py:131
  104.8 1.6 multiply_add_fusion.5
  106.3 1.2 multiply_subtract_fusion.3
  107.6 1.4 multiply_add_fusion.6
  112.9 1.6 multiply_add_fusion.5
  114.5 1.2 multiply_subtract_fusion.3
  115.7 1.4 multiply_add_fusion.6
  121.1 1.6 multiply_add_fusion.5
  122.7 1.2 multiply_subtract_fusion.3
  123.9 1.4 multiply_add_fusion.6
  129.3 1.6 multiply_add_fusion.5
  130.9 1.2 multiply_subtract_fusion.3
  132.1 1.4 multiply_add_fusion.6
  134.4 1.0 add_add_fusion.2
  137.5 1.6 multiply_add_fusion.5
  139.1 1.2 multiply_subtract_fusion.3
  140.3 1.4 multiply_add_fusion.6
  142.6 1.0 add_add_fusion.2
  145.7 1.6 multiply_add_fusion.5
  147.2 1.2 multiply_subtract_fusion.3
  148.5 1.4 multiply_add_fusion.6
  153.9 1.6 multiply_add_fusion.5
  155.4 1.2 multiply_subtract_fusion.3
  156.7 1.4 multiply_add_fusion.6
  162.0 1.6 multiply_add_fusion.5
  163.6 1.2 multiply_subtract_fusion.3
  164.9 1.4 multiply_add_fusion.6
  170.2 1.6 multiply_add_fusion.5
  171.8 1.2 multiply_subtract_fusion.3
  173.0 1.4 multiply_add_fusion.6
  178.4 1.6 multiply_add_fusion.5
  180.0 1.2 multiply_subtract_fusion.3
  181.2 1.4 multiply_add_fusion.6
  186.6 1.6 multiply_add_fusion.5
  188.2 1.2 multiply_subtract_fusion.3
  189.4 1.4 multiply_add_fusion.6
  194.8 1.6 multiply_add_fusion.5
  196.4 1.2 multiply_subtract_fusion.3
  197.6 1.4 multiply_add_fusion.6
  203.0 1.6 multiply_add_fusion.5
  204.5 1.2 multiply_subtract_fusion.3
  205.8 1.4 multiply_add_fusion.6
  211.2 1.6 multiply_add_fusion.5
  212.7 1.2 multiply_subtract_fusion.3
  214.0 1.4 multiply_add_fusion.6
  219.3 1.6 multiply_add_fusion.5
  220.9 1.2 multiply_subtract_fusion.3
  222.2 1.4 multiply_add_fusion.6
  227.5 1.6 multiply_add_fusion.5
  229.1 1.2 multiply_subtract_fusion.3
  230.3 1.4 multiply_add_fusion.6
  234.5 1.3 fusion.77
  235.9 1.4 fusion.78
  237.2 1.9 fusion.87
  (211 shorter events, 70.5 us)
Async XLA Ops:
  6.5 43.9 %copy-start = (bf16[2048,512]{1,0:T(8,128)(2,1)S(1)}, bf16[2048,512]{1,0:T(8,128)(2,1)}, u32[]{:S(2)}) copy-start(bf16[2048,512]{1,0:T(8,128)(2,1)} %param.10) | copy-start | bytes 6291460
  8.9 23.9 %all-to-all-start = ((bf16[8,128,512]{1,2,0:T(8,128)(2,1)}), bf16[8,128,512]{1,2,0:T(8,128)(2,1)S(1)}, u32[]{:S(2)}, u32[]{:S(2)}) async-start(bf16[8,128,512]{1,2,0:T(8,128)(2,1)} %stack.71), calls=%async_computation | async-start | bytes 2097152 | tf_op jit(solution)/shard_map/all_to_all | solution.py:31
  15.8 17.0 %copy-start.3 = (f32[7,3,512]{2,0,1:T(8,128)S(1)}, f32[7,3,512]{2,0,1:T(8,128)}, u32[]{:S(2)}) copy-start(f32[7,3,512]{2,0,1:T(8,128)} %param.9) | copy-start | bytes 129028
  15.8 86.1 %all-gather.3.cloned.1.call-start = ((), (), s32[]{:S(2)}) async-start(), calls=%async_computation.1 | async-start | bytes 2228224 | tf_op jit(solution)/shard_map/all_gather | solution.py:122
  41.7 0.8 copy-start.2
  42.5 5.6 %collective-permute-start = (bf16[6,3,512]{2,0,1:T(8,128)(2,1)S(1)}, bf16[6,3,512]{2,0,1:T(8,128)(2,1)S(1)}, u32[]{:S(2)}, u32[]{:S(2)}) collective-permute-start(bf16[6,3,512]{2,0,1:T(8,128)(2,1)S(1)} %bitcast.152), channel_id=1, source_target_pairs={{0,8},{8,16},{16,24},{24,32},{32,40},{40,48},{48,56},{56,64},{64,7... | collective-permute-start | bytes 55304 | tf_op jit(solution)/shard_map/ppermute | solution.py:13
  48.8 0.9 copy-start.1
Sparse Core Ops, SparseCore 0:
  50.6 51.2 all-gather.2
